TPU v7x, 32 devices: a whole 2x2x4 slice. The times are simulated.
32 devices in a mesh: chan: 8 (over y, x, core), band: 4 (over z).
Axes of the slice: x: 2, y: 2, z: 4, core: 2. Of those that a mesh axis runs over, the one named last changes fastest.
Arguments:
- spectra: bfloat16 [96, 2048, 384], P('band', 'chan')
- half_width: int32 [2048], P('chan'), may hold values from 4 to 12
- partner: int32 [2, 8], replicated, may hold values from 0 to 7, as said below
Outputs:
- cross: bfloat16 [3, 96, 2048, 512], P(None, 'band', 'chan')
Inputs may be any that keep to these rules, and one draw needn't show every extreme that they name: Each row pairs the blocks: partner[r, partner[r, a]] = a and partner[r, a] != a; no two rows pair the same two blocks.
All inputs are finite; a program needn't handle non-finite values.
Results may differ from a plain program's by a relative error of at most 0.0056.
Values may be sent and summed in bfloat16 or wider, within the bound.
No kernel may reach another device: no remote copies, remote signals or barrier semaphores. Data moves between devices by JAX's collectives and lax.ppermute only.
A program may use at most 128 MiB of HBM per device.

v0:
```python
import jax
import jax.numpy as jnp
from jax import lax
from jax.sharding import PartitionSpec as P

HMAX = 12
ROUNDS = 2


def padded_2(cells, sides, width):
    for axis, dim in sides:
        count = lax.axis_size(axis)
        ends = count - 1
        head = lax.slice_in_dim(cells, 0, width, axis=dim)
        tail = lax.slice_in_dim(cells, cells.shape[dim] - width, cells.shape[dim], axis=dim)
        cells = jnp.concatenate(
            [
                lax.ppermute(tail, axis, [(i, (i + 1) % count) for i in range(ends)]),
                cells,
                lax.ppermute(head, axis, [((i + 1) % count, i) for i in range(ends)]),
            ],
            axis=dim,
        )
    return cells


def pair_block(own, other, windows):
    turned = jnp.concatenate([-other[:, :, windows:], other[:, :, :windows]], axis=2)
    right = jnp.concatenate([other, turned], axis=1)
    product = jnp.einsum("fcw,fdw->fcd", own, right, preferred_element_type=jnp.float32)
    return (product * (1.0 / windows)).astype(jnp.bfloat16)


def body(spectra, half_width, partner):
    bins, chans, columns = spectra.shape
    windows = columns // 2
    raw = spectra.astype(jnp.float32)
    power = jnp.sum(raw * raw, axis=2)
    padded = padded_2(power, (("band", 0),), HMAX)
    first = lax.axis_index("band") * bins - HMAX
    position = first + jnp.arange(bins + 2 * HMAX, dtype=jnp.int32)
    present = ((position >= 0) & (position < bins * lax.axis_size("band"))).astype(jnp.float32)[
        :, None
    ]
    total = jnp.zeros((bins, chans), jnp.float32)
    count = jnp.zeros((bins, chans), jnp.float32)
    for offset in range(-HMAX, HMAX + 1):
        inside = (abs(offset) <= half_width).astype(jnp.float32)[None, :]
        total = total + padded[HMAX + offset : HMAX + offset + bins] * inside
        count = count + present[HMAX + offset : HMAX + offset + bins] * inside
    scale = lax.rsqrt(total / (2.0 * windows * count) + 1e-06)
    white = (raw * scale[:, :, None]).astype(jnp.bfloat16)
    blocks = lax.axis_size("chan")
    piece = chans // blocks
    sectioned = white.reshape(bins, blocks, piece, columns)
    results = [pair_block(white, white, windows)]
    for step in range(ROUNDS):
        held = lax.all_to_all(sectioned, "chan", split_axis=1, concat_axis=1, tiled=True)
        chosen = jnp.take(held, partner[step], axis=1)
        other = lax.all_to_all(chosen, "chan", split_axis=1, concat_axis=1, tiled=True)
        results.append(pair_block(white, other.reshape(bins, chans, columns), windows))
    return jnp.stack(results)


def solution(mesh):
    placed = (P("band", "chan", None), P("chan"), P())
    return jax.shard_map(
        body, mesh=mesh, in_specs=placed, out_specs=P(None, "band", "chan", None), check_vma=False
    )
```

profile of v0, /device:TPU:0, one launch (start us, length us, event | category | flops | bytes accessed | tf_op | source)
XLA Modules:
  0.0 252.5 jit_solution(4837852159365645081)
XLA Ops:
  0.0 0.0 copy-start.3
  0.0 3.4 %fusion = f32[24,256]{1,0:T(8,128)S(1)} fusion(bf16[24,256,384]{2,1,0:T(8,128)(2,1)} %param.5), kind=kLoop, calls=%fused_computation.8 | loop fusion | flops 7071744 | bytes 4743168 | tf_op jit(solution)/shard_map/reduce_sum | solution.py:38
  3.4 5.0 %collective-permute-start = (f32[12,256]{1,0:T(8,128)S(1)}, f32[12,256]{1,0:T(8,128)S(1)}, u32[]{:S(2)}, u32[]{:S(2)}) collective-permute-start(f32[12,256]{1,0:T(8,128)S(1)} %get-tuple-element.16), channel_id=1, source_target_pairs={{0,1},{1,2},{2,3},{4,5},{5,6},{6,7},{8,9},{9,10},{10,11},{12,13},{... | collective-permute-start | bytes 36872 | tf_op jit(solution)/shard_map/ppermute | solution.py:18
  8.3 1.3 collective-permute-start.1
  9.7 0.1 fusion.106
  9.7 0.0 copy-done.3
  9.8 0.1 fusion.107
  9.8 0.0 collective-permute-done
  9.8 4.1 %collective-permute-done.1 = f32[12,256]{1,0:T(8,128)S(1)} collective-permute-done((f32[12,256]{1,0:T(8,128)S(1)}, f32[12,256]{1,0:T(8,128)S(1)}, u32[]{:S(2)}, u32[]{:S(2)}) %collective-permute-start.1) | collective-permute-done | bytes 12320 | tf_op jit(solution)/shard_map/ppermute | solution.py:20
  14.0 0.2 fusion.101
  14.2 2.9 %fusion.1 = bf16[24,256,384]{2,1,0:T(8,128)(2,1)S(1)} fusion(bf16[24,256,384]{2,1,0:T(8,128)(2,1)} %param.5, f32[24,256]{1,0:T(8,128)S(1)} %fusion.101), kind=kLoop, calls=%fused_computation.9 | loop fusion | flops 7077888 | bytes 9461760 | tf_op jit(solution)/shard_map/convert_element_type | solution.py:52
  17.1 0.0 copy-start
  17.1 2.2 copy-done
  19.3 2.7 %copy.6 = bf16[24,8,32,384]{3,2,0,1:T(8,128)(2,1)} copy(bf16[24,8,32,384]{3,2,1,0:T(8,128)(2,1)S(1)} %bitcast.22) | data formatting | bytes 9437184 | tf_op jit(solution)/shard_map/reshape | solution.py:55
  22.0 0.0 copy-start.4
  22.0 4.7 %all-to-all-start = ((bf16[24,8,32,384]{3,2,0,1:T(8,128)(2,1)}), bf16[24,8,32,384]{3,2,0,1:T(8,128)(2,1)}, u32[]{:S(2)}, u32[]{:S(2)}) async-start(bf16[24,8,32,384]{3,2,0,1:T(8,128)(2,1)} %copy.6), calls=%async_computation | async-start | bytes 9437184 | tf_op jit(solution)/shard_map/all_to_all | solution.py:58
  26.7 0.0 copy-done.4
  26.8 54.7 %all-to-all-done = bf16[24,8,32,384]{3,2,0,1:T(8,128)(2,1)} async-done(((bf16[24,8,32,384]{3,2,0,1:T(8,128)(2,1)}), bf16[24,8,32,384]{3,2,0,1:T(8,128)(2,1)}, u32[]{:S(2)}, u32[]{:S(2)}) %all-to-all-start) | async-done | bytes 4718624 | tf_op jit(solution)/shard_map/all_to_all | solution.py:58
  81.4 5.7 %gather_fusion = bf16[8,24,32,384]{3,2,1,0:T(8,128)(2,1)} fusion(bf16[24,8,32,384]{3,2,0,1:T(8,128)(2,1)} %all-to-all-done, s32[1024]{0:T(1024)S(1)} %pad_clamp_fusion.1), kind=kCustom, calls=%fused_computation.clone | custom fusion | bytes 9437216 | tf_op jit(solution)/shard_map/jit(_take)/gather | solution.py:59
  87.1 5.1 %select_bitcast_fusion.1 = bf16[24,8,32,384]{3,2,0,1:T(8,128)(2,1)} fusion(bf16[8,24,32,384]{3,2,1,0:T(8,128)(2,1)} %gather_fusion, pred[8]{0:T(512)(128)(4,1)S(1)} %get-tuple-element.6), kind=kLoop, calls=%fused_computation.32 | loop fusion | flops 2359296 | bytes 9437192 | tf_op jit(solution)/shard_map/jit(_take)/select_n | solution.py:59
  92.2 4.6 %all-to-all-start.1 = ((bf16[24,8,32,384]{3,2,0,1:T(8,128)(2,1)}), bf16[24,8,32,384]{3,2,0,1:T(8,128)(2,1)}, u32[]{:S(2)}, u32[]{:S(2)}) async-start(bf16[24,8,32,384]{3,2,0,1:T(8,128)(2,1)} %select_bitcast_fusion.1), calls=%async_computation.1 | async-start | bytes 9437184 | tf_op jit(solution)/shard_map/all_to_all | solution.py:60
  96.8 5.8 %gather_fusion.1 = bf16[8,24,32,384]{3,2,1,0:T(8,128)(2,1)} fusion(bf16[24,8,32,384]{3,2,0,1:T(8,128)(2,1)} %all-to-all-done, s32[1024]{0:T(1024)S(1)} %pad_clamp_fusion), kind=kCustom, calls=%fused_computation.1.clone | custom fusion | bytes 9437216 | tf_op jit(solution)/shard_map/jit(_take)/gather | solution.py:59
  102.6 5.2 %select_bitcast_fusion = bf16[24,8,32,384]{3,2,0,1:T(8,128)(2,1)} fusion(bf16[8,24,32,384]{3,2,1,0:T(8,128)(2,1)} %gather_fusion.1, pred[8]{0:T(512)(128)(4,1)S(1)} %get-tuple-element.18), kind=kLoop, calls=%fused_computation.31 | loop fusion | flops 2359296 | bytes 9437192 | tf_op jit(solution)/shard_map/jit(_take)/select_n | solution.py:59
  107.8 43.7 %all-to-all-done.1 = bf16[24,8,32,384]{3,2,0,1:T(8,128)(2,1)} async-done(((bf16[24,8,32,384]{3,2,0,1:T(8,128)(2,1)}), bf16[24,8,32,384]{3,2,0,1:T(8,128)(2,1)}, u32[]{:S(2)}, u32[]{:S(2)}) %all-to-all-start.1) | async-done | bytes 4718624 | tf_op jit(solution)/shard_map/all_to_all | solution.py:60
  151.5 0.0 slice-start
  151.5 4.9 %all-to-all-start.2 = ((bf16[24,8,32,384]{3,2,0,1:T(8,128)(2,1)}), bf16[24,8,32,384]{3,2,0,1:T(8,128)(2,1)}, u32[]{:S(2)}, u32[]{:S(2)}) async-start(bf16[24,8,32,384]{3,2,0,1:T(8,128)(2,1)} %select_bitcast_fusion), calls=%async_computation.2 | async-start | bytes 9437184 | tf_op jit(solution)/shard_map/all_to_all | solution.py:60
  156.5 0.0 slice-start.1
  156.5 6.6 %slice_negate_fusion.2 = (bf16[24,256,192]{2,1,0:T(8,128)(2,1)}, bf16[24,256,192]{2,1,0:T(8,128)(2,1)}) fusion(bf16[24,256,384]{2,1,0:T(8,128)(2,1)} %copy-done), kind=kLoop, calls=%fused_computation.35 | loop fusion | flops 1179648 | bytes 9437184 | tf_op jit(solution)/shard_map/neg | solution.py:28
  163.1 0.0 slice-done
  163.1 0.0 slice-done.1
  163.1 8.0 %fusion.20 = bf16[1,24,256,512]{3,2,1,0:T(8,128)(2,1)} fusion(bf16[24,256,384]{2,1,0:T(8,128)(2,1)S(1)} %bitcast.24, bf16[24,256,192]{2,1,0:T(8,128)(2,1)} %get-tuple-element.11, bf16[24,256,192]{2,1,0:T(8,128)(2,1)} %get-tuple-element.10), kind=kOutput, calls=%fused_computation.28 | convolution fusion | flops 2450522112 | bytes 15728640 | tf_op jit(solution)/shard_map/fcw,fdw->fcd/dot_general | solution.py:30
  171.2 3.2 %copy.7 = bf16[24,8,32,384]{3,2,1,0:T(8,128)(2,1)S(1)} copy(bf16[24,8,32,384]{3,2,0,1:T(8,128)(2,1)} %all-to-all-done.1) | data formatting | bytes 9437184 | tf_op jit(solution)/shard_map/all_to_all | solution.py:60
  174.4 0.0 copy-start.1
  174.4 2.2 copy-done.1
  176.5 3.7 %slice_negate_fusion.1 = (bf16[24,256,192]{2,1,0:T(8,128)(2,1)}, bf16[24,256,192]{2,1,0:T(8,128)(2,1)}) fusion(bf16[24,256,384]{2,1,0:T(8,128)(2,1)S(1)} %bitcast.27), kind=kLoop, calls=%fused_computation.34 | loop fusion | flops 1179648 | bytes 9437184 | tf_op jit(solution)/shard_map/neg | solution.py:28
  180.3 30.7 %all-to-all-done.2 = bf16[24,8,32,384]{3,2,0,1:T(8,128)(2,1)} async-done(((bf16[24,8,32,384]{3,2,0,1:T(8,128)(2,1)}), bf16[24,8,32,384]{3,2,0,1:T(8,128)(2,1)}, u32[]{:S(2)}, u32[]{:S(2)}) %all-to-all-start.2) | async-done | bytes 4718624 | tf_op jit(solution)/shard_map/all_to_all | solution.py:60
  211.0 0.0 slice-start.2
  211.0 3.3 %copy.8 = bf16[24,8,32,384]{3,2,1,0:T(8,128)(2,1)S(1)} copy(bf16[24,8,32,384]{3,2,0,1:T(8,128)(2,1)} %all-to-all-done.2) | data formatting | bytes 9437184 | tf_op jit(solution)/shard_map/all_to_all | solution.py:60
  214.3 0.0 copy-start.2
  214.4 0.0 slice-start.3
  214.4 4.0 %slice_negate_fusion = (bf16[24,256,192]{2,1,0:T(8,128)(2,1)}, bf16[24,256,192]{2,1,0:T(8,128)(2,1)}) fusion(bf16[24,256,384]{2,1,0:T(8,128)(2,1)S(1)} %bitcast.29), kind=kLoop, calls=%fused_computation.33 | loop fusion | flops 1179648 | bytes 9437184 | tf_op jit(solution)/shard_map/neg | solution.py:28
  218.4 0.0 copy-done.2
  218.4 0.0 slice-done.2
  218.4 0.0 slice-done.3
  218.4 8.8 %fusion.21 = bf16[1,24,256,512]{3,2,1,0:T(8,128)(2,1)} fusion(bf16[24,256,384]{2,1,0:T(8,128)(2,1)S(1)} %bitcast.26, bf16[24,256,192]{2,1,0:T(8,128)(2,1)} %get-tuple-element.13, bf16[24,256,192]{2,1,0:T(8,128)(2,1)} %get-tuple-element.12, bf16[24,256,384]{2,1,0:T(8,128)(2,1)} %bitcast.28), kind=kOutput, calls=%fused_computation.29 | convolution fusion | flops 2450522112 | bytes 20447232 | tf_op jit(solution)/shard_map/fcw,fdw->fcd/dot_general | solution.py:30
  227.2 8.8 %fusion.22 = bf16[1,24,256,512]{3,2,1,0:T(8,128)(2,1)} fusion(bf16[24,256,384]{2,1,0:T(8,128)(2,1)S(1)} %bitcast.26, bf16[24,256,192]{2,1,0:T(8,128)(2,1)} %get-tuple-element.15, bf16[24,256,192]{2,1,0:T(8,128)(2,1)} %get-tuple-element.14, bf16[24,256,384]{2,1,0:T(8,128)(2,1)} %bitcast.30), kind=kOutput, calls=%fused_computation.30 | convolution fusion | flops 2450522112 | bytes 20447232 | tf_op jit(solution)/shard_map/fcw,fdw->fcd/dot_general | solution.py:30
  236.0 16.5 %pad_maximum_fusion = bf16[3,24,256,512]{3,2,1,0:T(8,128)(2,1)} fusion(bf16[1,24,256,512]{3,2,1,0:T(8,128)(2,1)} %fusion.22, bf16[1,24,256,512]{3,2,1,0:T(8,128)(2,1)} %fusion.21, bf16[1,24,256,512]{3,2,1,0:T(8,128)(2,1)} %fusion.20), kind=kLoop, calls=%fused_computation.2 | loop fusion | flops 18874368 | bytes 37748736 | tf_op jit(solution)/shard_map/stack | solution.py:62
  (8 shorter events, 0.0 us)
Async XLA Ops:
  0.0 9.7 %copy-start.3 = (s32[256]{0:T(256)S(1)}, s32[256]{0:T(256)}, u32[]{:S(2)}) copy-start(s32[256]{0:T(256)} %param.6) | copy-start | bytes 3076
  3.4 6.5 %collective-permute-start = (f32[12,256]{1,0:T(8,128)S(1)}, f32[12,256]{1,0:T(8,128)S(1)}, u32[]{:S(2)}, u32[]{:S(2)}) collective-permute-start(f32[12,256]{1,0:T(8,128)S(1)} %get-tuple-element.16), channel_id=1, source_target_pairs={{0,1},{1,2},{2,3},{4,5},{5,6},{6,7},{8,9},{9,10},{10,11},{12,13},{... | collective-permute-start | bytes 36872 | tf_op jit(solution)/shard_map/ppermute | solution.py:18
  8.3 5.6 %collective-permute-start.1 = (f32[12,256]{1,0:T(8,128)S(1)}, f32[12,256]{1,0:T(8,128)S(1)}, u32[]{:S(2)}, u32[]{:S(2)}) collective-permute-start(f32[12,256]{1,0:T(8,128)S(1)} %get-tuple-element.17), channel_id=1, source_target_pairs={{1,0},{2,1},{3,2},{5,4},{6,5},{7,6},{9,8},{10,9},{11,10},{13,12},{... | collective-permute-start | bytes 36872 | tf_op jit(solution)/shard_map/ppermute | solution.py:20
  17.1 2.2 copy-start
  22.0 4.8 %copy-start.4 = (s32[2,8]{1,0:T(2,128)S(1)}, s32[2,8]{1,0:T(2,128)}, u32[]{:S(2)}) copy-start(s32[2,8]{1,0:T(2,128)} %param.7) | copy-start | bytes 196
  22.0 59.5 %all-to-all-start = ((bf16[24,8,32,384]{3,2,0,1:T(8,128)(2,1)}), bf16[24,8,32,384]{3,2,0,1:T(8,128)(2,1)}, u32[]{:S(2)}, u32[]{:S(2)}) async-start(bf16[24,8,32,384]{3,2,0,1:T(8,128)(2,1)} %copy.6), calls=%async_computation | async-start | bytes 9437184 | tf_op jit(solution)/shard_map/all_to_all | solution.py:58
  92.2 59.3 %all-to-all-start.1 = ((bf16[24,8,32,384]{3,2,0,1:T(8,128)(2,1)}), bf16[24,8,32,384]{3,2,0,1:T(8,128)(2,1)}, u32[]{:S(2)}, u32[]{:S(2)}) async-start(bf16[24,8,32,384]{3,2,0,1:T(8,128)(2,1)} %select_bitcast_fusion.1), calls=%async_computation.1 | async-start | bytes 9437184 | tf_op jit(solution)/shard_map/all_to_all | solution.py:60
  151.5 11.6 %slice-start = ((s8[4718592]{0:T(1024)(128)(4,1)}), s8[524288]{0:T(1024)(128)(4,1)S(1)}, s32[]{:S(2)}) async-start(s8[4718592]{0:T(1024)(128)(4,1)} %bitcast.23), calls=%async_computation.3 | async-start | bytes 1048576
  151.5 59.5 %all-to-all-start.2 = ((bf16[24,8,32,384]{3,2,0,1:T(8,128)(2,1)}), bf16[24,8,32,384]{3,2,0,1:T(8,128)(2,1)}, u32[]{:S(2)}, u32[]{:S(2)}) async-start(bf16[24,8,32,384]{3,2,0,1:T(8,128)(2,1)} %select_bitcast_fusion), calls=%async_computation.2 | async-start | bytes 9437184 | tf_op jit(solution)/shard_map/all_to_all | solution.py:60
  156.5 6.7 %slice-start.1 = ((s8[4718592]{0:T(1024)(128)(4,1)}), s8[4194304]{0:T(1024)(128)(4,1)S(1)}, s32[]{:S(2)}) async-start(s8[4718592]{0:T(1024)(128)(4,1)} %bitcast.23), calls=%async_computation.4 | async-start | bytes 8388608
  174.4 2.2 copy-start.1
  211.0 7.4 %slice-start.2 = ((s8[4718592]{0:T(1024)(128)(4,1)}), s8[4194304]{0:T(1024)(128)(4,1)S(1)}, s32[]{:S(2)}) async-start(s8[4718592]{0:T(1024)(128)(4,1)} %bitcast.25), calls=%async_computation.5 | async-start | bytes 8388608
  214.3 4.1 %copy-start.2 = (bf16[24,8,32,384]{3,2,1,0:T(8,128)(2,1)}, bf16[24,8,32,384]{3,2,1,0:T(8,128)(2,1)S(1)}, u32[]{:S(2)}) copy-start(bf16[24,8,32,384]{3,2,1,0:T(8,128)(2,1)S(1)} %copy.8) | copy-start | bytes 14155780
  214.4 4.1 %slice-start.3 = ((s8[4718592]{0:T(1024)(128)(4,1)}), s8[524288]{0:T(1024)(128)(4,1)S(1)}, s32[]{:S(2)}) async-start(s8[4718592]{0:T(1024)(128)(4,1)} %bitcast.25), calls=%async_computation.6 | async-start | bytes 1048576
where the time goes:
time: 253 us
  waiting for transfers between devices  133 us (53%)
  other arithmetic  47.6 us (19%)
  matrix products  25.6 us (10%)
  local copies, waits for them, and re-layouts  25.3 us (10%)
  starting transfers between devices  20.5 us (8%)
    all_to_all x2, waiting for transfers between devices, body(): lax.all_to_all(chosen, 'chan', split_axis=1, concat_axis=1, tiled=True)  74.5 us
    all_to_all x1, waiting for transfers between devices, body(): lax.all_to_all(sectioned, 'chan', split_axis=1, concat_axis=1, tiled=True)  54.7 us
    dot_general x3, matrix products, pair_block(): jnp.einsum('fcw,fdw->fcd', own, right, preferred_element_type=jnp.float32)  25.6 us
    another operation x1, other arithmetic, body(): return jnp.stack(results)  16.5 us
    neg x3, other arithmetic, pair_block(): -other[:, :, windows:]  14.4 us
    gather x2, local copies, waits for them, and re-layouts, body(): chosen = jnp.take(held, partner[step], axis=1)  11.5 us
    select_n x2, other arithmetic, body(): chosen = jnp.take(held, partner[step], axis=1)  10.2 us
    all_to_all x2, starting transfers between devices, body(): lax.all_to_all(chosen, 'chan', split_axis=1, concat_axis=1, tiled=True)  9.53 us
  transfers between devices with their start and end apart: 5, of which 4 were waited for; matrix products, arithmetic and copies ran while one was open for 13% of the time, Pallas kernels for 0%

commit v1 on v0

--- a/solution.py
+++ b/solution.py
@@ -5,6 +5,17 @@
 
 HMAX = 12
 ROUNDS = 2
+
+
+def split_up(array, dim, size):
+    before, after = (array.shape[:dim], array.shape[dim + 1 :])
+    return jnp.moveaxis(array.reshape(*before, size, -1, *after), dim, 0)
+
+
+def laid_out(blocks, dim):
+    blocks = jnp.moveaxis(blocks, 0, dim)
+    shape = blocks.shape
+    return blocks.reshape(*shape[:dim], shape[dim] * shape[dim + 1], *shape[dim + 2 :])
 
 
 def padded_2(cells, sides, width):
@@ -57,7 +68,14 @@
     for step in range(ROUNDS):
         held = lax.all_to_all(sectioned, "chan", split_axis=1, concat_axis=1, tiled=True)
         chosen = jnp.take(held, partner[step], axis=1)
-        other = lax.all_to_all(chosen, "chan", split_axis=1, concat_axis=1, tiled=True)
+        length, index = (lax.axis_size("chan"), lax.axis_index("chan"))
+        tiles = split_up(chosen, 1, length)
+        outs = [tiles[index]]
+        for step_2 in range(1, length):
+            sent = tiles[index ^ step_2]
+            outs.append(lax.ppermute(sent, "chan", [(i_2, i_2 ^ step_2) for i_2 in range(length)]))
+        tiles = jnp.stack(outs)[index ^ jnp.arange(length)]
+        other = laid_out(tiles, 1)
         results.append(pair_block(white, other.reshape(bins, chans, columns), windows))
     return jnp.stack(results)
 

time: 253 us -> 304 us (1.20)
  local copies, waits for them, and re-layouts: 25.3 us -> 62.2 us
  waiting for transfers between devices: 133 us -> 148 us
  other arithmetic: 47.6 us -> 44.5 us
    ppermute x0 -> x14, waiting for transfers between devices: none -> 95.3 us  [body(): lax.ppermute(sent, 'chan', [(i_2, i_2 ^ step_2) for i_2 in range(length)])]
    all_to_all x2 -> x0, waiting for transfers between devices: 74.5 us -> none  [body(): lax.all_to_all(chosen, 'chan', split_axis=1, concat_axis=1, tiled=True)]
    unnamed x18 -> x40, local copies, waits for them, and re-layouts: 4.39 us -> 21.1 us
    ppermute x0 -> x14, starting transfers between devices: none -> 12.1 us  [body(): lax.ppermute(sent, 'chan', [(i_2, i_2 ^ step_2) for i_2 in range(length)])]
    gather x0 -> x2, local copies, waits for them, and re-layouts: none -> 11.4 us  [body(): tiles = jnp.stack(outs)[index ^ jnp.arange(length)]]
    all_to_all x2 -> x0, starting transfers between devices: 9.53 us -> none  [body(): lax.all_to_all(chosen, 'chan', split_axis=1, concat_axis=1, tiled=True)]
    transpose x0 -> x2, local copies, waits for them, and re-layouts: none -> 8.67 us  [laid_out(): blocks = jnp.moveaxis(blocks, 0, dim)]
    all_to_all x1, waiting for transfers between devices: 54.7 us -> 48.1 us  [body(): lax.all_to_all(sectioned, 'chan', split_axis=1, concat_axis=1, tiled=True)]
  transfers between devices with their start and end apart: 5 -> 17, of which waited for: 4 -> 6; matrix products, arithmetic and copies ran while one was open for 13% -> 15% of each run, Pallas kernels for 0% -> 0%
where the time goes in v1:
time: 304 us; the launch traced here: 303 us
  waiting for transfers between devices  148 us (49%)
  local copies, waits for them, and re-layouts  62.2 us (20%)
  other arithmetic  44.5 us (15%)
  matrix products  25.6 us (8%)
  starting transfers between devices  23.1 us (8%)
    ppermute x14, waiting for transfers between devices, body(): lax.ppermute(sent, 'chan', [(i_2, i_2 ^ step_2) for i_2 in range(length)])  95.3 us
    all_to_all x1, waiting for transfers between devices, body(): lax.all_to_all(sectioned, 'chan', split_axis=1, concat_axis=1, tiled=True)  48.1 us
    dot_general x3, matrix products, pair_block(): jnp.einsum('fcw,fdw->fcd', own, right, preferred_element_type=jnp.float32)  25.6 us
    unnamed x40, local copies, waits for them, and re-layouts  21.1 us
    another operation x1, other arithmetic, body(): return jnp.stack(results)  16.5 us
    neg x3, other arithmetic, pair_block(): -other[:, :, windows:]  14.4 us
    ppermute x14, starting transfers between devices, body(): lax.ppermute(sent, 'chan', [(i_2, i_2 ^ step_2) for i_2 in range(length)])  12.1 us
    gather x2, local copies, waits for them, and re-layouts, body(): chosen = jnp.take(held, partner[step], axis=1)  11.4 us
  transfers between devices with their start and end apart: 17, of which 6 were waited for; matrix products, arithmetic and copies ran while one was open for 15% of the time, Pallas kernels for 0%

profile of v1, /device:TPU:0, one launch (start us, length us, event | category | flops | bytes accessed | tf_op | source)
XLA Modules:
  0.0 303.2 jit_solution(1399749733346042968)
XLA Ops:
  0.0 3.4 %fusion = f32[24,256]{1,0:T(8,128)S(1)} fusion(bf16[24,256,384]{2,1,0:T(8,128)(2,1)} %param.5), kind=kLoop, calls=%fused_computation.10 | loop fusion | flops 7071744 | bytes 4743168 | tf_op jit(solution)/shard_map/reduce_sum | solution.py:49
  3.4 5.0 %collective-permute-start = (f32[12,256]{1,0:T(8,128)S(1)}, f32[12,256]{1,0:T(8,128)S(1)}, u32[]{:S(2)}, u32[]{:S(2)}) collective-permute-start(f32[12,256]{1,0:T(8,128)S(1)} %get-tuple-element.30), channel_id=1, source_target_pairs={{0,1},{1,2},{2,3},{4,5},{5,6},{6,7},{8,9},{9,10},{10,11},{12,13},{... | collective-permute-start | bytes 36872 | tf_op jit(solution)/shard_map/ppermute | solution.py:29
  8.3 1.3 collective-permute-start.1
  9.7 0.1 fusion.107
  9.8 0.1 fusion.108
  9.8 4.1 %collective-permute-done.1 = f32[12,256]{1,0:T(8,128)S(1)} collective-permute-done((f32[12,256]{1,0:T(8,128)S(1)}, f32[12,256]{1,0:T(8,128)S(1)}, u32[]{:S(2)}, u32[]{:S(2)}) %collective-permute-start.1) | collective-permute-done | bytes 12320 | tf_op jit(solution)/shard_map/ppermute | solution.py:31
  14.0 0.2 fusion.101
  14.2 2.9 fusion.1
  17.1 0.0 copy-start
  17.1 2.2 copy-done
  19.3 2.7 copy.6
  22.0 4.7 %all-to-all-start = ((bf16[24,8,32,384]{3,2,0,1:T(8,128)(2,1)}), bf16[24,8,32,384]{3,2,0,1:T(8,128)(2,1)}, u32[]{:S(2)}, u32[]{:S(2)}) async-start(bf16[24,8,32,384]{3,2,0,1:T(8,128)(2,1)} %copy.6), calls=%async_computation | async-start | bytes 9437184 | tf_op jit(solution)/shard_map/all_to_all | solution.py:69
  26.9 6.5 %slice_negate_fusion.2 = (bf16[24,256,192]{2,1,0:T(8,128)(2,1)}, bf16[24,256,192]{2,1,0:T(8,128)(2,1)}) fusion(bf16[24,256,384]{2,1,0:T(8,128)(2,1)} %copy-done), kind=kLoop, calls=%fused_computation.37 | loop fusion | flops 1179648 | bytes 9437184 | tf_op jit(solution)/shard_map/neg | solution.py:39
  33.3 48.1 %all-to-all-done = bf16[24,8,32,384]{3,2,0,1:T(8,128)(2,1)} async-done(((bf16[24,8,32,384]{3,2,0,1:T(8,128)(2,1)}), bf16[24,8,32,384]{3,2,0,1:T(8,128)(2,1)}, u32[]{:S(2)}, u32[]{:S(2)}) %all-to-all-start) | async-done | bytes 4718624 | tf_op jit(solution)/shard_map/all_to_all | solution.py:69
  81.4 5.6 %gather_fusion.3 = bf16[8,24,32,384]{3,2,1,0:T(8,128)(2,1)} fusion(bf16[24,8,32,384]{3,2,0,1:T(8,128)(2,1)} %all-to-all-done, s32[1024]{0:T(1024)S(1)} %pad_clamp_fusion), kind=kCustom, calls=%fused_computation.1.clone | custom fusion | bytes 9437216 | tf_op jit(solution)/shard_map/jit(_take)/gather | solution.py:70
  87.1 5.8 %gather_fusion.2 = bf16[8,24,32,384]{3,2,1,0:T(8,128)(2,1)} fusion(bf16[24,8,32,384]{3,2,0,1:T(8,128)(2,1)} %all-to-all-done, s32[1024]{0:T(1024)S(1)} %pad_clamp_fusion.2), kind=kCustom, calls=%fused_computation.clone | custom fusion | bytes 9437216 | tf_op jit(solution)/shard_map/jit(_take)/gather | solution.py:70
  92.9 7.1 %select_bitcast_fusion = (bf16[24,8,32,384]{3,2,0,1:T(8,128)(2,1)S(1)}, bf16[24,8,32,384]{3,2,0,1:T(8,128)(2,1)}) fusion(bf16[8,24,32,384]{3,2,1,0:T(8,128)(2,1)} %gather_fusion.3, pred[8]{0:T(512)(128)(4,1)S(1)} %get-tuple-element.32, bf16[8,24,32,384]{3,2,1,0:T(8,128)(2,1)} %gather_fusion.2, pred[8]{0:T(512)(128)(4,1)S(1)} %get-tuple-element.6), kind=kLoop, calls=%fused_computation.33 | loop fusion | flops 4718592 | bytes 18874384 | tf_op jit(solution)/shard_map/jit(_take)/select_n | solution.py:70
  100.0 2.2 copy-done.2
  102.2 2.1 constant_dynamic-slice_fusion
  104.3 8.1 %fusion.20 = bf16[1,24,256,512]{3,2,1,0:T(8,128)(2,1)} fusion(bf16[24,256,384]{2,1,0:T(8,128)(2,1)S(1)} %bitcast.66, bf16[24,256,192]{2,1,0:T(8,128)(2,1)} %get-tuple-element.11, bf16[24,256,192]{2,1,0:T(8,128)(2,1)} %get-tuple-element.10), kind=kOutput, calls=%fused_computation.30 | convolution fusion | flops 2450522112 | bytes 15728640 | tf_op jit(solution)/shard_map/fcw,fdw->fcd/dot_general | solution.py:41
  112.3 0.7 collective-permute-start.15
  113.0 2.3 collective-permute-start.14
  115.4 1.4 collective-permute-start.10
  116.7 1.9 bitcast_dynamic-update-slice_fusion.7
  118.7 2.9 constant_dynamic-slice_fusion.7
  121.6 1.9 bitcast_dynamic-update-slice_fusion.15
  123.5 0.0 collective-permute-done.9
  123.5 0.5 collective-permute-start.12
  124.0 2.0 bitcast_dynamic-update-slice_fusion.6
  126.0 40.1 %collective-permute-done.10 = bf16[24,1,32,384]{3,2,0,1:T(8,128)(2,1)S(1)} collective-permute-done((bf16[24,1,32,384]{3,2,0,1:T(8,128)(2,1)}, bf16[24,1,32,384]{3,2,0,1:T(8,128)(2,1)S(1)}, u32[]{:S(2)}, u32[]{:S(2)}) %collective-permute-start.10) | collective-permute-done | bytes 589856 | tf_op jit(solution)/shard_map/ppermute | solution.py:76
  166.1 0.5 collective-permute-start.13
  166.7 0.9 bitcast_dynamic-update-slice_fusion.5
  167.6 1.3 collective-permute-start.8
  168.9 0.9 bitcast_dynamic-update-slice_fusion.4
  169.7 2.3 collective-permute-start.7
  172.1 0.9 bitcast_dynamic-update-slice_fusion.3
  173.0 34.0 %collective-permute-done.13 = bf16[24,1,32,384]{3,2,0,1:T(8,128)(2,1)S(1)} collective-permute-done((bf16[24,1,32,384]{3,2,0,1:T(8,128)(2,1)S(1)}, bf16[24,1,32,384]{3,2,0,1:T(8,128)(2,1)S(1)}, u32[]{:S(2)}, u32[]{:S(2)}) %collective-permute-start.13) | collective-permute-done | bytes 589856 | tf_op jit(solution)/shard_map/ppermute | solution.py:76
  207.0 0.1 collective-permute-start.2
  207.1 0.9 bitcast_dynamic-update-slice_fusion.2
  208.0 0.6 collective-permute-start.3
  208.6 0.9 bitcast_dynamic-update-slice_fusion.1
  209.5 1.1 collective-permute-start.4
  210.6 0.9 bitcast_dynamic-update-slice_fusion
  211.6 1.2 collective-permute-start.5
  212.7 0.9 bitcast_dynamic-update-slice_fusion.14
  213.6 10.6 %collective-permute-done.3 = bf16[24,1,32,384]{3,2,0,1:T(8,128)(2,1)S(1)} collective-permute-done((bf16[24,1,32,384]{3,2,0,1:T(8,128)(2,1)S(1)}, bf16[24,1,32,384]{3,2,0,1:T(8,128)(2,1)S(1)}, u32[]{:S(2)}, u32[]{:S(2)}) %collective-permute-start.3) | collective-permute-done | bytes 589856 | tf_op jit(solution)/shard_map/ppermute | solution.py:76
  224.2 0.9 bitcast_dynamic-update-slice_fusion.13
  225.1 10.6 %collective-permute-done.4 = bf16[24,1,32,384]{3,2,0,1:T(8,128)(2,1)S(1)} collective-permute-done((bf16[24,1,32,384]{3,2,0,1:T(8,128)(2,1)S(1)}, bf16[24,1,32,384]{3,2,0,1:T(8,128)(2,1)S(1)}, u32[]{:S(2)}, u32[]{:S(2)}) %collective-permute-start.4) | collective-permute-done | bytes 589856 | tf_op jit(solution)/shard_map/ppermute | solution.py:76
  235.7 1.0 bitcast_dynamic-update-slice_fusion.12
  236.7 0.9 bitcast_dynamic-update-slice_fusion.11
  237.5 5.7 %gather_fusion.1 = bf16[8,24,32,384]{3,2,1,0:T(8,128)(2,1)} fusion(bf16[8,24,32,384]{3,2,1,0:T(8,128)(2,1)} %bitcast.28, s32[1024]{0:T(1024)S(1)} %pad_clamp_fusion.1), kind=kCustom, calls=%fused_computation.3 | custom fusion | bytes 9437216 | tf_op jit(solution)/shard_map/gather | solution.py:77
  243.2 5.3 %copy.8 = bf16[24,8,1,32,384]{4,3,1,0,2:T(8,128)(2,1)} copy(bf16[24,8,1,32,384]{4,3,0,1,2:T(8,128)(2,1)} %bitcast.76) | data formatting | bytes 9437184 | tf_op jit(solution)/shard_map/transpose | solution.py:16
  248.6 0.9 bitcast_dynamic-update-slice_fusion.10
  249.4 0.9 bitcast_dynamic-update-slice_fusion.9
  250.3 0.9 bitcast_dynamic-update-slice_fusion.8
  251.2 5.7 %gather_fusion = bf16[8,24,32,384]{3,2,1,0:T(8,128)(2,1)} fusion(bf16[8,24,32,384]{3,2,1,0:T(8,128)(2,1)} %bitcast.12, s32[1024]{0:T(1024)S(1)} %pad_clamp_fusion.1), kind=kCustom, calls=%fused_computation.2 | custom fusion | bytes 9437216 | tf_op jit(solution)/shard_map/gather | solution.py:77
  256.9 3.3 %copy.7 = bf16[24,8,1,32,384]{4,3,1,0,2:T(8,128)(2,1)S(1)} copy(bf16[24,8,1,32,384]{4,3,0,1,2:T(8,128)(2,1)} %bitcast.75) | data formatting | bytes 9437184 | tf_op jit(solution)/shard_map/transpose | solution.py:16
  260.2 0.0 slice-start.2
  260.3 4.1 %slice_negate_fusion.1 = (bf16[24,256,192]{2,1,0:T(8,128)(2,1)}, bf16[24,256,192]{2,1,0:T(8,128)(2,1)}) fusion(bf16[24,256,384]{2,1,0:T(8,128)(2,1)S(1)} %bitcast.73), kind=kLoop, calls=%fused_computation.36 | loop fusion | flops 1179648 | bytes 9437184 | tf_op jit(solution)/shard_map/neg | solution.py:39
  264.4 1.0 copy-done.1
  265.3 3.8 %slice_negate_fusion = (bf16[24,256,192]{2,1,0:T(8,128)(2,1)}, bf16[24,256,192]{2,1,0:T(8,128)(2,1)}) fusion(bf16[24,256,384]{2,1,0:T(8,128)(2,1)S(1)} %bitcast.72), kind=kLoop, calls=%fused_computation.35 | loop fusion | flops 1179648 | bytes 9437184 | tf_op jit(solution)/shard_map/neg | solution.py:39
  269.2 8.8 %fusion.21 = bf16[1,24,256,512]{3,2,1,0:T(8,128)(2,1)} fusion(bf16[24,256,384]{2,1,0:T(8,128)(2,1)S(1)} %bitcast.68, bf16[24,256,192]{2,1,0:T(8,128)(2,1)} %get-tuple-element.13, bf16[24,256,192]{2,1,0:T(8,128)(2,1)} %get-tuple-element.12, bf16[24,256,384]{2,1,0:T(8,128)(2,1)} %bitcast.74), kind=kOutput, calls=%fused_computation.31 | convolution fusion | flops 2450522112 | bytes 20447232 | tf_op jit(solution)/shard_map/fcw,fdw->fcd/dot_general | solution.py:41
  278.0 8.8 %fusion.22 = bf16[1,24,256,512]{3,2,1,0:T(8,128)(2,1)} fusion(bf16[24,256,384]{2,1,0:T(8,128)(2,1)S(1)} %bitcast.68, bf16[24,256,192]{2,1,0:T(8,128)(2,1)} %get-tuple-element.22, bf16[24,256,192]{2,1,0:T(8,128)(2,1)} %get-tuple-element.21, bf16[24,256,384]{2,1,0:T(8,128)(2,1)} %bitcast.69), kind=kOutput, calls=%fused_computation.32 | convolution fusion | flops 2450522112 | bytes 20447232 | tf_op jit(solution)/shard_map/fcw,fdw->fcd/dot_general | solution.py:41
  286.7 16.5 %pad_maximum_fusion = bf16[3,24,256,512]{3,2,1,0:T(8,128)(2,1)} fusion(bf16[1,24,256,512]{3,2,1,0:T(8,128)(2,1)} %fusion.22, bf16[1,24,256,512]{3,2,1,0:T(8,128)(2,1)} %fusion.21, bf16[1,24,256,512]{3,2,1,0:T(8,128)(2,1)} %fusion.20), kind=kLoop, calls=%fused_computation.4 | loop fusion | flops 18874368 | bytes 37748736 | tf_op jit(solution)/shard_map/stack | solution.py:80
  (45 shorter events, 0.1 us)
Async XLA Ops:
  0.0 9.7 %copy-start.5 = (s32[256]{0:T(256)S(1)}, s32[256]{0:T(256)}, u32[]{:S(2)}) copy-start(s32[256]{0:T(256)} %param.6) | copy-start | bytes 3076
  3.4 6.5 %collective-permute-start = (f32[12,256]{1,0:T(8,128)S(1)}, f32[12,256]{1,0:T(8,128)S(1)}, u32[]{:S(2)}, u32[]{:S(2)}) collective-permute-start(f32[12,256]{1,0:T(8,128)S(1)} %get-tuple-element.30), channel_id=1, source_target_pairs={{0,1},{1,2},{2,3},{4,5},{5,6},{6,7},{8,9},{9,10},{10,11},{12,13},{... | collective-permute-start | bytes 36872 | tf_op jit(solution)/shard_map/ppermute | solution.py:29
  8.3 5.6 %collective-permute-start.1 = (f32[12,256]{1,0:T(8,128)S(1)}, f32[12,256]{1,0:T(8,128)S(1)}, u32[]{:S(2)}, u32[]{:S(2)}) collective-permute-start(f32[12,256]{1,0:T(8,128)S(1)} %get-tuple-element.31), channel_id=1, source_target_pairs={{1,0},{2,1},{3,2},{5,4},{6,5},{7,6},{9,8},{10,9},{11,10},{13,12},{... | collective-permute-start | bytes 36872 | tf_op jit(solution)/shard_map/ppermute | solution.py:31
  17.1 2.2 copy-start
  22.0 4.8 %copy-start.6 = (s32[2,8]{1,0:T(2,128)S(1)}, s32[2,8]{1,0:T(2,128)}, u32[]{:S(2)}) copy-start(s32[2,8]{1,0:T(2,128)} %param.7) | copy-start | bytes 196
  22.0 59.5 %all-to-all-start = ((bf16[24,8,32,384]{3,2,0,1:T(8,128)(2,1)}), bf16[24,8,32,384]{3,2,0,1:T(8,128)(2,1)}, u32[]{:S(2)}, u32[]{:S(2)}) async-start(bf16[24,8,32,384]{3,2,0,1:T(8,128)(2,1)} %copy.6), calls=%async_computation | async-start | bytes 9437184 | tf_op jit(solution)/shard_map/all_to_all | solution.py:69
  87.1 17.2 %slice-start = ((s8[4718592]{0:T(1024)(128)(4,1)}), s8[524288]{0:T(1024)(128)(4,1)S(1)}, s32[]{:S(2)}) async-start(s8[4718592]{0:T(1024)(128)(4,1)} %bitcast.65), calls=%async_computation.1 | async-start | bytes 1048576
  92.9 11.4 %slice-start.1 = ((s8[4718592]{0:T(1024)(128)(4,1)}), s8[4194304]{0:T(1024)(128)(4,1)S(1)}, s32[]{:S(2)}) async-start(s8[4718592]{0:T(1024)(128)(4,1)} %bitcast.65), calls=%async_computation.2 | async-start | bytes 8388608
  100.0 2.2 copy-start.2
  104.3 19.2 %collective-permute-start.9 = (bf16[24,1,32,384]{3,2,0,1:T(8,128)(2,1)}, bf16[24,1,32,384]{3,2,0,1:T(8,128)(2,1)}, u32[]{:S(2)}, u32[]{:S(2)}) collective-permute-start(bf16[24,1,32,384]{3,2,0,1:T(8,128)(2,1)} %get-tuple-element.29), channel_id=1, source_target_pairs={{0,4},{4,0},{8,12},{12,8},{16,20},{20,16},{24,28},{28,24},{1,5},{5... | collective-permute-start | bytes 1769480 | tf_op jit(solution)/shard_map/ppermute | solution.py:76
  112.3 97.1 %collective-permute-start.15 = (bf16[24,1,32,384]{3,2,0,1:T(8,128)(2,1)}, bf16[24,1,32,384]{3,2,0,1:T(8,128)(2,1)S(1)}, u32[]{:S(2)}, u32[]{:S(2)}) collective-permute-start(bf16[24,1,32,384]{3,2,0,1:T(8,128)(2,1)} %get-tuple-element.23), channel_id=1, source_target_pairs={{0,28},{4,24},{8,20},{12,16},{16,12},{20,8},{24,4},{28,0},{1,29},{... | collective-permute-start | bytes 1769480 | tf_op jit(solution)/shard_map/ppermute | solution.py:76
  113.0 95.0 %collective-permute-start.14 = (bf16[24,1,32,384]{3,2,0,1:T(8,128)(2,1)}, bf16[24,1,32,384]{3,2,0,1:T(8,128)(2,1)S(1)}, u32[]{:S(2)}, u32[]{:S(2)}) collective-permute-start(bf16[24,1,32,384]{3,2,0,1:T(8,128)(2,1)} %get-tuple-element.24), channel_id=1, source_target_pairs={{0,24},{4,28},{8,16},{12,20},{16,8},{20,12},{24,0},{28,4},{1,25},{... | collective-permute-start | bytes 1769480 | tf_op jit(solution)/shard_map/ppermute | solution.py:76
  115.4 52.2 %collective-permute-start.11 = (bf16[24,1,32,384]{3,2,0,1:T(8,128)(2,1)}, bf16[24,1,32,384]{3,2,0,1:T(8,128)(2,1)S(1)}, u32[]{:S(2)}, u32[]{:S(2)}) collective-permute-start(bf16[24,1,32,384]{3,2,0,1:T(8,128)(2,1)} %get-tuple-element.27), channel_id=1, source_target_pairs={{0,12},{4,8},{8,4},{12,0},{16,28},{20,24},{24,20},{28,16},{1,13},{... | collective-permute-start | bytes 1769480 | tf_op jit(solution)/shard_map/ppermute | solution.py:76
  115.4 50.8 %collective-permute-start.10 = (bf16[24,1,32,384]{3,2,0,1:T(8,128)(2,1)}, bf16[24,1,32,384]{3,2,0,1:T(8,128)(2,1)S(1)}, u32[]{:S(2)}, u32[]{:S(2)}) collective-permute-start(bf16[24,1,32,384]{3,2,0,1:T(8,128)(2,1)} %get-tuple-element.28), channel_id=1, source_target_pairs={{0,8},{4,12},{8,0},{12,4},{16,24},{20,28},{24,16},{28,20},{1,9},{5... | collective-permute-start | bytes 1769480 | tf_op jit(solution)/shard_map/ppermute | solution.py:76
  118.7 4.8 %copy-start.4 = (bf16[24,1,32,384]{3,2,0,1:T(8,128)(2,1)S(1)}, bf16[24,1,32,384]{3,2,0,1:T(8,128)(2,1)}, u32[]{:S(2)}) copy-start(bf16[24,1,32,384]{3,2,0,1:T(8,128)(2,1)} %get-tuple-element.26) | copy-start | bytes 1769476
  118.7 47.4 %copy-start.3 = (bf16[24,1,32,384]{3,2,0,1:T(8,128)(2,1)S(1)}, bf16[24,1,32,384]{3,2,0,1:T(8,128)(2,1)}, u32[]{:S(2)}) copy-start(bf16[24,1,32,384]{3,2,0,1:T(8,128)(2,1)} %get-tuple-element.25) | copy-start | bytes 1769476
  123.5 46.2 %collective-permute-start.12 = (bf16[24,1,32,384]{3,2,0,1:T(8,128)(2,1)S(1)}, bf16[24,1,32,384]{3,2,0,1:T(8,128)(2,1)S(1)}, u32[]{:S(2)}, u32[]{:S(2)}) collective-permute-start(bf16[24,1,32,384]{3,2,0,1:T(8,128)(2,1)S(1)} %copy-done.4), channel_id=1, source_target_pairs={{0,16},{4,20},{8,24},{12,28},{16,0},{20,4},{24,8},{28,12},{1,17},{... | collective-permute-start | bytes 1769480 | tf_op jit(solution)/shard_map/ppermute | solution.py:76
  166.1 40.9 %collective-permute-start.13 = (bf16[24,1,32,384]{3,2,0,1:T(8,128)(2,1)S(1)}, bf16[24,1,32,384]{3,2,0,1:T(8,128)(2,1)S(1)}, u32[]{:S(2)}, u32[]{:S(2)}) collective-permute-start(bf16[24,1,32,384]{3,2,0,1:T(8,128)(2,1)S(1)} %copy-done.3), channel_id=1, source_target_pairs={{0,20},{4,16},{8,28},{12,24},{16,4},{20,0},{24,12},{28,8},{1,21},{... | collective-permute-start | bytes 1769480 | tf_op jit(solution)/shard_map/ppermute | solution.py:76
  167.6 82.7 %collective-permute-start.8 = (bf16[24,1,32,384]{3,2,0,1:T(8,128)(2,1)S(1)}, bf16[24,1,32,384]{3,2,0,1:T(8,128)(2,1)S(1)}, u32[]{:S(2)}, u32[]{:S(2)}) collective-permute-start(bf16[24,1,32,384]{3,2,0,1:T(8,128)(2,1)S(1)} %get-tuple-element.14), channel_id=1, source_target_pairs={{0,28},{4,24},{8,20},{12,16},{16,12},{20,8},{24,4},{28,0},{1,29},{... | collective-permute-start | bytes 1769480 | tf_op jit(solution)/shard_map/ppermute | solution.py:76
  169.7 79.7 %collective-permute-start.7 = (bf16[24,1,32,384]{3,2,0,1:T(8,128)(2,1)S(1)}, bf16[24,1,32,384]{3,2,0,1:T(8,128)(2,1)S(1)}, u32[]{:S(2)}, u32[]{:S(2)}) collective-permute-start(bf16[24,1,32,384]{3,2,0,1:T(8,128)(2,1)S(1)} %get-tuple-element.15), channel_id=1, source_target_pairs={{0,24},{4,28},{8,16},{12,20},{16,8},{20,12},{24,0},{28,4},{1,25},{... | collective-permute-start | bytes 1769480 | tf_op jit(solution)/shard_map/ppermute | solution.py:76
  207.0 4.6 %collective-permute-start.2 = (bf16[24,1,32,384]{3,2,0,1:T(8,128)(2,1)S(1)}, bf16[24,1,32,384]{3,2,0,1:T(8,128)(2,1)S(1)}, u32[]{:S(2)}, u32[]{:S(2)}) collective-permute-start(bf16[24,1,32,384]{3,2,0,1:T(8,128)(2,1)S(1)} %get-tuple-element.20), channel_id=1, source_target_pairs={{0,4},{4,0},{8,12},{12,8},{16,20},{20,16},{24,28},{28,24},{1,5},{5... | collective-permute-start | bytes 1769480 | tf_op jit(solution)/shard_map/ppermute | solution.py:76
  208.0 16.2 %collective-permute-start.3 = (bf16[24,1,32,384]{3,2,0,1:T(8,128)(2,1)S(1)}, bf16[24,1,32,384]{3,2,0,1:T(8,128)(2,1)S(1)}, u32[]{:S(2)}, u32[]{:S(2)}) collective-permute-start(bf16[24,1,32,384]{3,2,0,1:T(8,128)(2,1)S(1)} %get-tuple-element.19), channel_id=1, source_target_pairs={{0,8},{4,12},{8,0},{12,4},{16,24},{20,28},{24,16},{28,20},{1,9},{5... | collective-permute-start | bytes 1769480 | tf_op jit(solution)/shard_map/ppermute | solution.py:76
  209.5 26.2 %collective-permute-start.4 = (bf16[24,1,32,384]{3,2,0,1:T(8,128)(2,1)S(1)}, bf16[24,1,32,384]{3,2,0,1:T(8,128)(2,1)S(1)}, u32[]{:S(2)}, u32[]{:S(2)}) collective-permute-start(bf16[24,1,32,384]{3,2,0,1:T(8,128)(2,1)S(1)} %get-tuple-element.18), channel_id=1, source_target_pairs={{0,12},{4,8},{8,4},{12,0},{16,28},{20,24},{24,20},{28,16},{1,13},{... | collective-permute-start | bytes 1769480 | tf_op jit(solution)/shard_map/ppermute | solution.py:76
  211.6 25.1 %collective-permute-start.5 = (bf16[24,1,32,384]{3,2,0,1:T(8,128)(2,1)S(1)}, bf16[24,1,32,384]{3,2,0,1:T(8,128)(2,1)S(1)}, u32[]{:S(2)}, u32[]{:S(2)}) collective-permute-start(bf16[24,1,32,384]{3,2,0,1:T(8,128)(2,1)S(1)} %get-tuple-element.17), channel_id=1, source_target_pairs={{0,16},{4,20},{8,24},{12,28},{16,0},{20,4},{24,8},{28,12},{1,17},{... | collective-permute-start | bytes 1769480 | tf_op jit(solution)/shard_map/ppermute | solution.py:76
  224.2 24.4 %collective-permute-start.6 = (bf16[24,1,32,384]{3,2,0,1:T(8,128)(2,1)S(1)}, bf16[24,1,32,384]{3,2,0,1:T(8,128)(2,1)S(1)}, u32[]{:S(2)}, u32[]{:S(2)}) collective-permute-start(bf16[24,1,32,384]{3,2,0,1:T(8,128)(2,1)S(1)} %get-tuple-element.16), channel_id=1, source_target_pairs={{0,20},{4,16},{8,28},{12,24},{16,4},{20,0},{24,12},{28,8},{1,21},{... | collective-permute-start | bytes 1769480 | tf_op jit(solution)/shard_map/ppermute | solution.py:76
  256.9 8.5 %slice-start.4 = ((s8[4718592]{0:T(1024)(128)(4,1)}), s8[4194304]{0:T(1024)(128)(4,1)S(1)}, s32[]{:S(2)}) async-start(s8[4718592]{0:T(1024)(128)(4,1)} %bitcast.70), calls=%async_computation.5 | async-start | bytes 8388608
  260.2 5.1 %copy-start.1 = (bf16[24,8,1,32,384]{4,3,1,0,2:T(8,128)(2,1)}, bf16[24,8,1,32,384]{4,3,1,0,2:T(8,128)(2,1)S(1)}, u32[]{:S(2)}) copy-start(bf16[24,8,1,32,384]{4,3,1,0,2:T(8,128)(2,1)S(1)} %copy.7) | copy-start | bytes 14155780
  260.2 5.1 %slice-start.5 = ((s8[4718592]{0:T(1024)(128)(4,1)}), s8[524288]{0:T(1024)(128)(4,1)S(1)}, s32[]{:S(2)}) async-start(s8[4718592]{0:T(1024)(128)(4,1)} %bitcast.70), calls=%async_computation.6 | async-start | bytes 1048576
  260.2 8.9 %slice-start.2 = ((s8[4718592]{0:T(1024)(128)(4,1)}), s8[4194304]{0:T(1024)(128)(4,1)S(1)}, s32[]{:S(2)}) async-start(s8[4718592]{0:T(1024)(128)(4,1)} %bitcast.67), calls=%async_computation.3 | async-start | bytes 8388608
  265.3 3.8 %slice-start.3 = ((s8[4718592]{0:T(1024)(128)(4,1)}), s8[524288]{0:T(1024)(128)(4,1)S(1)}, s32[]{:S(2)}) async-start(s8[4718592]{0:T(1024)(128)(4,1)} %bitcast.67), calls=%async_computation.4 | async-start | bytes 1048576
